TPU v7x, 512 devices: a whole 4x8x8 slice. The times are simulated.
512 devices in a mesh: wide: 64 (over z, y_hi, core), narrow: 8 (over x, y_lo).
Axes of the slice: x: 4, y: 8 (y_hi: 4, y_lo: 2; y = y_hi * 2 + y_lo), z: 8, core: 2. Of those that a mesh axis runs over, the one named last changes fastest.
Arguments:
- positions: float32 [3, 131072], P(None, ('wide', 'narrow')), may hold values from 0 to 1
- volumes: float32 [131072], P(('wide', 'narrow')), may hold values from 0.5 to 2
- phase_field: float32 [131072], P(('wide', 'narrow')), may hold values from -1 to 1.4
- stencil_weights: float32 [64, 131072], P(None, ('wide', 'narrow')), may hold values from 0.005 to 0.05
- stencil_slots: int32 [64, 131072], P(None, ('wide', 'narrow')), may hold values from 0 to 767, as said below
- send_lists: int32 [2, 131072], P(None, ('wide', 'narrow')), may hold values from 0 to 255, as said below
Outputs:
- phase_next: float32 [131072], P(('wide', 'narrow'))
- potential_next: float32 [131072], P(('wide', 'narrow'))
Inputs may be any that keep to these rules, and one draw needn't show every extreme that they name: `stencil_slots`: entry k of point i names a neighbour in ext of i's block: values below 256 are rows of the same block other than i; 256 + s is slot s of the list that the block one lower along wide (cyclically) sends up, 512 + s slot s of the list that the block one higher sends down; s is always below that list's count c, and every slot below c is named by some point of the receiving block. `send_lists`: each block's list in each row has a count c of 1 to 256: its first c slots hold distinct rows of 0 to 255 and the rest hold 0; in each row some block's list is full.
All inputs are finite; a program needn't handle non-finite values.
Results may differ from a plain program's by a relative error of at most 0.00002.
Values sent between devices are 32-bit elements; how exact they have to be, the bound alone decides.
A program may use at most 64 MiB of HBM per device.

v0:
```python
import jax
import jax.numpy as jnp
from jax import lax
from jax.sharding import PartitionSpec as P

kernel_strength = 0.1
gradient_energy = 0.5
time_step = 0.2


def padded(cells, sides, width):
    for axis, dim in sides:
        count = lax.axis_size(axis)
        head = lax.slice_in_dim(cells, 0, width, axis=dim)
        tail = lax.slice_in_dim(cells, cells.shape[dim] - width, cells.shape[dim], axis=dim)
        cells = jnp.concatenate(
            [
                lax.ppermute(tail, axis, [(i, (i + 1) % count) for i in range(count)]),
                cells,
                lax.ppermute(head, axis, [((i + 1) % count, i) for i in range(count)]),
            ],
            axis=dim,
        )
    return cells


def add_sources(totals, targets, sources, vols, values, kernel_decay):
    count_src = values.shape[0]
    block_len = 512

    def add_block(turn, partial_sums):
        offset = turn * block_len
        src_block = lax.dynamic_slice_in_dim(sources, offset, block_len, 1)
        vol_block = lax.dynamic_slice_in_dim(vols, offset, block_len, 0)
        val_block = lax.dynamic_slice_in_dim(values, offset, block_len, 0)
        distance = (targets[0][:, None] - src_block[0][None, :]) ** 2
        distance = distance + (targets[1][:, None] - src_block[1][None, :]) ** 2
        distance = distance + (targets[2][:, None] - src_block[2][None, :]) ** 2
        gauss_vol = jnp.exp(-kernel_decay * distance) * vol_block[None, :]
        return (
            partial_sums[0] + jnp.sum(gauss_vol, axis=1),
            partial_sums[1] + jnp.sum(gauss_vol * val_block[None, :], axis=1),
        )

    return lax.fori_loop(0, count_src // block_len, add_block, totals)


def shards(positions, volumes, phase_field, stencil_weights, stencil_slots, send_lists):
    own_rows = phase_field.shape[0]
    send_len = send_lists.shape[1]
    patch_len = own_rows * lax.axis_size("narrow")
    kernel_decay = 0.5 * float(patch_len) ** (2.0 / 3.0)
    packet_rows = jnp.concatenate([send_lists[1], send_lists[0]])

    def extend(field_now):
        rim_values = padded(field_now[packet_rows], (("wide", 0),), send_len)
        return jnp.concatenate([field_now, rim_values[:send_len], rim_values[-send_len:]])

    zero_sums = (jnp.zeros((own_rows,), jnp.float32), jnp.zeros((own_rows,), jnp.float32))

    def kernel_totals(field_now):
        stacked = jnp.concatenate([positions, volumes[None, :], field_now[None, :]], axis=0)
        part_rows = lax.all_gather(stacked, "narrow", axis=1, tiled=True)
        return add_sources(
            zero_sums, positions, part_rows[:3], part_rows[3], part_rows[4], kernel_decay
        )

    def laplace(field_now):
        extended = extend(field_now)
        neighbour_vals = extended[stencil_slots]
        return jnp.sum(stencil_weights * (neighbour_vals - field_now[None, :]), axis=0)

    def potential(field_now):
        sum_mass, sum_field = kernel_totals(field_now)
        kernel_term = kernel_strength * sum_mass * field_now - kernel_strength * sum_field
        return field_now**3 - field_now + kernel_term - gradient_energy * laplace(field_now)

    potential_now = potential(phase_field)
    phase_next = phase_field + time_step * laplace(potential_now)
    return (phase_next, potential(phase_next))


def solution(mesh):
    placed = (
        P(None, ("wide", "narrow")),
        P(("wide", "narrow")),
        P(("wide", "narrow")),
        P(None, ("wide", "narrow")),
        P(None, ("wide", "narrow")),
        P(None, ("wide", "narrow")),
    )
    return jax.shard_map(
        shards,
        mesh=mesh,
        in_specs=placed,
        out_specs=(P(("wide", "narrow")), P(("wide", "narrow"))),
        check_vma=False,
    )
```

profile of v0, /device:TPU:8, one launch (start us, length us, event | category | flops | bytes accessed | tf_op | source)
XLA Modules:
  0.0 310.8 jit_solution(3009720424811803415)
XLA Ops:
  0.6 0.8 slice_bitcast_fusion.1
  1.4 0.7 copy-done
  2.1 3.5 %gather_fusion = f32[512]{0:T(512)S(1)} fusion(f32[256]{0:T(256)S(1)} %copy-done, s32[1024]{0:T(1024)S(1)} %pad_clamp_fusion), kind=kCustom, calls=%fused_computation | custom fusion | bytes 6144 | tf_op jit(solution)/shard_map/gather | solution.py:56
  5.6 1.9 collective-permute-start
  7.5 13.2 %collective-permute-start.1 = (f32[256]{0:T(256)S(1)}, f32[256]{0:T(256)S(1)}, u32[]{:S(2)}, u32[]{:S(2)}) collective-permute-start(f32[256]{0:T(256)S(1)} %get-tuple-element.361), channel_id=1, source_target_pairs={{8,0},{16,8},{24,16},{32,24},{40,32},{48,40},{56,48},{64,56},{72,6... | collective-permute-start | bytes 3080 | tf_op jit(solution)/shard_map/ppermute | solution.py:20
  20.7 0.7 copy-done.6
  21.4 28.3 %all_gather.6 = f32[5,2048]{1,0:T(8,128)S(1)} all-gather(f32[5,256]{1,0:T(8,128)S(1)} %pad_maximum_fusion), channel_id=1, replica_groups=mesh['wide'=64,'narrow'=8] {'narrow'}, dimensions={1}, use_global_device_ids=true | all-gather | bytes 46080 | tf_op jit(solution)/shard_map/all_gather | solution.py:63
  49.8 0.6 copy-done.4
  50.7 0.7 slice-done
  51.4 2.8 while.32
  51.6 0.4 multiply_reduce_fusion.7
  52.3 0.4 multiply_reduce_fusion.7
  53.0 0.4 multiply_reduce_fusion.7
  53.7 0.4 multiply_reduce_fusion.7
  54.2 65.3 %gather_fusion.1 = f32[16384]{0:T(1024)S(1)} fusion(f32[768]{0:T(1024)S(1)} %pad_maximum_fusion.2, s32[16384]{0:T(1024)S(1)} %broadcast_clamp_fusion), kind=kCustom, calls=%fused_computation.1 | custom fusion | bytes 196608 | tf_op jit(solution)/shard_map/gather | solution.py:70
  119.6 0.8 copy-done.2
  120.4 3.5 %gather_fusion.2 = f32[512]{0:T(512)S(1)} fusion(f32[256]{0:T(256)S(1)} %fusion.5, s32[1024]{0:T(1024)S(1)} %pad_clamp_fusion), kind=kCustom, calls=%fused_computation.2 | custom fusion | bytes 6144 | tf_op jit(solution)/shard_map/gather | solution.py:56
  123.9 1.9 collective-permute-start.2
  125.9 7.9 %collective-permute-start.3 = (f32[256]{0:T(256)S(1)}, f32[256]{0:T(256)S(1)}, u32[]{:S(2)}, u32[]{:S(2)}) collective-permute-start(f32[256]{0:T(256)S(1)} %get-tuple-element.359), channel_id=1, source_target_pairs={{8,0},{16,8},{24,16},{32,24},{40,32},{48,40},{56,48},{64,56},{72,6... | collective-permute-start | bytes 3080 | tf_op jit(solution)/shard_map/ppermute | solution.py:20
  133.8 1.2 collective-permute-done.3
  135.0 65.3 %gather_fusion.3 = f32[16384]{0:T(1024)S(1)} fusion(f32[768]{0:T(1024)S(1)} %pad_maximum_fusion.3, s32[16384]{0:T(1024)S(1)} %broadcast_clamp_fusion), kind=kCustom, calls=%fused_computation.3 | custom fusion | bytes 196608 | tf_op jit(solution)/shard_map/gather | solution.py:70
  200.4 28.3 %all_gather.7 = f32[5,2048]{1,0:T(8,128)S(1)} all-gather(f32[5,256]{1,0:T(8,128)S(1)} %fusion.3), channel_id=1, replica_groups=mesh['wide'=64,'narrow'=8] {'narrow'}, dimensions={1}, use_global_device_ids=true | all-gather | bytes 46080 | tf_op jit(solution)/shard_map/all_gather | solution.py:63
  228.7 3.5 %gather_fusion.4 = f32[512]{0:T(512)S(1)} fusion(f32[256]{0:T(256)S(1)} %multiply_add_fusion, s32[1024]{0:T(1024)S(1)} %pad_clamp_fusion), kind=kCustom, calls=%fused_computation.4 | custom fusion | bytes 6144 | tf_op jit(solution)/shard_map/gather | solution.py:56
  232.2 1.9 collective-permute-start.4
  234.1 7.9 %collective-permute-start.5 = (f32[256]{0:T(256)S(1)}, f32[256]{0:T(256)S(1)}, u32[]{:S(2)}, u32[]{:S(2)}) collective-permute-start(f32[256]{0:T(256)S(1)} %get-tuple-element.357), channel_id=1, source_target_pairs={{8,0},{16,8},{24,16},{32,24},{40,32},{48,40},{56,48},{64,56},{72,6... | collective-permute-start | bytes 3080 | tf_op jit(solution)/shard_map/ppermute | solution.py:20
  242.0 2.8 while.33
  242.3 0.4 multiply_reduce_fusion.8
  243.0 0.4 multiply_reduce_fusion.8
  243.7 0.4 multiply_reduce_fusion.8
  244.4 0.4 multiply_reduce_fusion.8
  244.9 65.3 %gather_fusion.5 = f32[16384]{0:T(1024)S(1)} fusion(f32[768]{0:T(1024)S(1)} %pad_maximum_fusion.4, s32[16384]{0:T(1024)S(1)} %broadcast_clamp_fusion), kind=kCustom, calls=%fused_computation.5 | custom fusion | bytes 196608 | tf_op jit(solution)/shard_map/gather | solution.py:70
  310.2 0.6 fusion.7
  (84 shorter events, 2.6 us)
Async XLA Ops:
  1.4 0.7 copy-start
  5.6 15.1 %copy-start.3 = (f32[3,256]{1,0:T(4,128)S(1)}, f32[3,256]{1,0:T(4,128)}, u32[]{:S(2)}) copy-start(f32[3,256]{1,0:T(4,128)} %param.10) | copy-start | bytes 9220
  5.6 48.6 %collective-permute-start = (f32[256]{0:T(256)S(1)}, f32[256]{0:T(256)S(1)}, u32[]{:S(2)}, u32[]{:S(2)}) collective-permute-start(f32[256]{0:T(256)S(1)} %get-tuple-element.360), channel_id=1, source_target_pairs={{0,8},{8,16},{16,24},{24,32},{32,40},{40,48},{48,56},{56,64},{64,7... | collective-permute-start | bytes 3080 | tf_op jit(solution)/shard_map/ppermute | solution.py:18
  7.5 46.7 %collective-permute-start.1 = (f32[256]{0:T(256)S(1)}, f32[256]{0:T(256)S(1)}, u32[]{:S(2)}, u32[]{:S(2)}) collective-permute-start(f32[256]{0:T(256)S(1)} %get-tuple-element.361), channel_id=1, source_target_pairs={{8,0},{16,8},{24,16},{32,24},{40,32},{48,40},{56,48},{64,56},{72,6... | collective-permute-start | bytes 3080 | tf_op jit(solution)/shard_map/ppermute | solution.py:20
  20.7 0.7 copy-start.6
  49.7 0.6 copy-start.4
  49.7 0.9 copy-start.5
  50.6 0.7 slice-start
  119.5 0.8 copy-start.2
  123.9 9.8 %collective-permute-start.2 = (f32[256]{0:T(256)S(1)}, f32[256]{0:T(256)S(1)}, u32[]{:S(2)}, u32[]{:S(2)}) collective-permute-start(f32[256]{0:T(256)S(1)} %get-tuple-element.358), channel_id=1, source_target_pairs={{0,8},{8,16},{16,24},{24,32},{32,40},{40,48},{48,56},{56,64},{64,7... | collective-permute-start | bytes 3080 | tf_op jit(solution)/shard_map/ppermute | solution.py:18
  125.9 9.1 %collective-permute-start.3 = (f32[256]{0:T(256)S(1)}, f32[256]{0:T(256)S(1)}, u32[]{:S(2)}, u32[]{:S(2)}) collective-permute-start(f32[256]{0:T(256)S(1)} %get-tuple-element.359), channel_id=1, source_target_pairs={{8,0},{16,8},{24,16},{32,24},{40,32},{48,40},{56,48},{64,56},{72,6... | collective-permute-start | bytes 3080 | tf_op jit(solution)/shard_map/ppermute | solution.py:20
  200.3 109.9 %copy-start.1 = (f32[256]{0:T(256)}, f32[256]{0:T(256)S(1)}, u32[]{:S(2)}) copy-start(f32[256]{0:T(256)S(1)} %multiply_add_fusion) | copy-start | bytes 3076
  232.2 12.7 %collective-permute-start.4 = (f32[256]{0:T(256)S(1)}, f32[256]{0:T(256)S(1)}, u32[]{:S(2)}, u32[]{:S(2)}) collective-permute-start(f32[256]{0:T(256)S(1)} %get-tuple-element.356), channel_id=1, source_target_pairs={{0,8},{8,16},{16,24},{24,32},{32,40},{40,48},{48,56},{56,64},{64,7... | collective-permute-start | bytes 3080 | tf_op jit(solution)/shard_map/ppermute | solution.py:18
  234.1 10.7 %collective-permute-start.5 = (f32[256]{0:T(256)S(1)}, f32[256]{0:T(256)S(1)}, u32[]{:S(2)}, u32[]{:S(2)}) collective-permute-start(f32[256]{0:T(256)S(1)} %get-tuple-element.357), channel_id=1, source_target_pairs={{8,0},{16,8},{24,16},{32,24},{40,32},{48,40},{56,48},{64,56},{72,6... | collective-permute-start | bytes 3080 | tf_op jit(solution)/shard_map/ppermute | solution.py:20
where the time goes:
time: 311 us
  local copies, waits for them, and re-layouts  213 us (68%)
  blocking collectives  56.6 us (18%)
  starting transfers between devices  34.7 us (11%)
  other arithmetic  4.31 us (1%)
    gather x6, local copies, waits for them, and re-layouts, laplace(): neighbour_vals = extended[stencil_slots]  196 us
    all_gather x2, blocking collectives, kernel_totals(): part_rows = lax.all_gather(stacked, 'narrow', axis=1, tiled=True)  56.6 us
    ppermute x3, starting transfers between devices, padded(): lax.ppermute(head, axis, [((i + 1) % count, i) for i in range(count)])  28.9 us
    gather x3, local copies, waits for them, and re-layouts, extend(): rim_values = padded(field_now[packet_rows], (('wide', 0),), send_len)  10.5 us
  transfers between devices with their start and end apart: 6, of which 1 were waited for; matrix products, arithmetic and copies ran while one was open for 2% of the time, Pallas kernels for 0%

commit v1 on v0

--- a/solution.py
+++ b/solution.py
@@ -60,7 +60,8 @@
 
     def kernel_totals(field_now):
         stacked = jnp.concatenate([positions, volumes[None, :], field_now[None, :]], axis=0)
-        part_rows = lax.all_gather(stacked, "narrow", axis=1, tiled=True)
+        repeated = jnp.stack([stacked] * lax.axis_size("narrow"))
+        part_rows = jnp.concatenate(lax.all_to_all(repeated, "narrow", 0, 0), axis=1)
         return add_sources(
             zero_sums, positions, part_rows[:3], part_rows[3], part_rows[4], kernel_decay
         )

time: 311 us -> 266 us (0.86)
  the two profiles are of different devices: /device:TPU:8 before, /device:TPU:2 now
where the time goes in v1:
time: 266 us
  local copies, waits for them, and re-layouts  212 us (80%)
  starting transfers between devices  46.3 us (17%)
  other arithmetic  4.3 us (2%)
    gather x6, local copies, waits for them, and re-layouts, laplace(): neighbour_vals = extended[stencil_slots]  196 us
    ppermute x3, starting transfers between devices, padded(): lax.ppermute(head, axis, [((i + 1) % count, i) for i in range(count)])  29.8 us
    all_to_all x2, starting transfers between devices, kernel_totals(): lax.all_to_all(repeated, 'narrow', 0, 0)  10.8 us
    gather x3, local copies, waits for them, and re-layouts, extend(): rim_values = padded(field_now[packet_rows], (('wide', 0),), send_len)  10.5 us
    ppermute x3, starting transfers between devices, padded(): lax.ppermute(tail, axis, [(i, (i + 1) % count) for i in range(count)])  5.76 us
  transfers between devices with their start and end apart: 8, of which 1 were waited for; matrix products, arithmetic and copies ran while one was open for 50% of the time, Pallas kernels for 0%

profile of v1, /device:TPU:2, one launch (start us, length us, event | category | flops | bytes accessed | tf_op | source)
XLA Modules:
  0.0 265.6 jit_solution(15991493932549470355)
XLA Ops:
  0.6 0.8 slice_bitcast_fusion.1
  1.4 0.7 copy-done
  2.1 3.5 %gather_fusion = f32[512]{0:T(512)S(1)} fusion(f32[256]{0:T(256)S(1)} %copy-done, s32[1024]{0:T(1024)S(1)} %pad_clamp_fusion), kind=kCustom, calls=%fused_computation | custom fusion | bytes 6144 | tf_op jit(solution)/shard_map/gather | solution.py:56
  5.6 1.9 collective-permute-start
  7.5 14.1 %collective-permute-start.1 = (f32[256]{0:T(256)S(1)}, f32[256]{0:T(256)S(1)}, u32[]{:S(2)}, u32[]{:S(2)}) collective-permute-start(f32[256]{0:T(256)S(1)} %get-tuple-element.361), channel_id=1, source_target_pairs={{8,0},{16,8},{24,16},{32,24},{40,32},{48,40},{56,48},{64,56},{72,6... | collective-permute-start | bytes 3080 | tf_op jit(solution)/shard_map/ppermute | solution.py:20
  21.6 0.7 copy-done.5
  22.3 0.6 stack.4
  22.9 5.1 %all-to-all-start = ((f32[8,5,256]{2,1,0:T(8,128)}), f32[8,5,256]{2,1,0:T(8,128)S(1)}, u32[]{:S(2)}, u32[]{:S(2)}) async-start(f32[8,5,256]{2,1,0:T(8,128)} %stack.4), calls=%async_computation | async-start | bytes 131072 | tf_op jit(solution)/shard_map/all_to_all | solution.py:64
  28.2 65.3 %gather_fusion.1 = f32[16384]{0:T(1024)S(1)} fusion(f32[768]{0:T(1024)S(1)} %pad_maximum_fusion.2, s32[16384]{0:T(1024)S(1)} %broadcast_clamp_fusion), kind=kCustom, calls=%fused_computation.1 | custom fusion | bytes 196608 | tf_op jit(solution)/shard_map/gather | solution.py:71
  93.5 0.8 copy-done.2
  94.3 2.8 %while.32 = (s32[]{:T(128)}, f32[256]{0:T(256)S(1)}, f32[256]{0:T(256)S(1)}, f32[3,256]{1,0:T(4,128)S(1)}, f32[3,2048]{1,0:T(4,128)S(1)}, /*index=5*/f32[2048]{0...) while((s32[]{:T(128)}, f32[256]{0:T(256)S(1)}, ...), condition=%wide.region_3.0_spmd.clone, body=%wide.region_0.0_spmd.clone.sunk | while | flops 1704457 | bytes 48361 | solution.py:45
  94.6 0.4 multiply_reduce_fusion.7
  95.3 0.4 multiply_reduce_fusion.7
  96.0 0.4 multiply_reduce_fusion.7
  96.7 0.4 multiply_reduce_fusion.7
  97.2 3.5 %gather_fusion.2 = f32[512]{0:T(512)S(1)} fusion(f32[256]{0:T(256)S(1)} %fusion.5, s32[1024]{0:T(1024)S(1)} %pad_clamp_fusion), kind=kCustom, calls=%fused_computation.2 | custom fusion | bytes 6144 | tf_op jit(solution)/shard_map/gather | solution.py:56
  100.7 1.9 collective-permute-start.2
  102.6 7.9 %collective-permute-start.3 = (f32[256]{0:T(256)S(1)}, f32[256]{0:T(256)S(1)}, u32[]{:S(2)}, u32[]{:S(2)}) collective-permute-start(f32[256]{0:T(256)S(1)} %get-tuple-element.359), channel_id=1, source_target_pairs={{8,0},{16,8},{24,16},{32,24},{40,32},{48,40},{56,48},{64,56},{72,6... | collective-permute-start | bytes 3080 | tf_op jit(solution)/shard_map/ppermute | solution.py:20
  110.5 1.2 collective-permute-done.3
  111.8 65.3 %gather_fusion.3 = f32[16384]{0:T(1024)S(1)} fusion(f32[768]{0:T(1024)S(1)} %pad_maximum_fusion.3, s32[16384]{0:T(1024)S(1)} %broadcast_clamp_fusion), kind=kCustom, calls=%fused_computation.3 | custom fusion | bytes 196608 | tf_op jit(solution)/shard_map/gather | solution.py:71
  177.1 3.5 %gather_fusion.4 = f32[512]{0:T(512)S(1)} fusion(f32[256]{0:T(256)S(1)} %multiply_add_fusion, s32[1024]{0:T(1024)S(1)} %pad_clamp_fusion), kind=kCustom, calls=%fused_computation.4 | custom fusion | bytes 6144 | tf_op jit(solution)/shard_map/gather | solution.py:56
  180.7 1.9 collective-permute-start.4
  182.6 7.9 %collective-permute-start.5 = (f32[256]{0:T(256)S(1)}, f32[256]{0:T(256)S(1)}, u32[]{:S(2)}, u32[]{:S(2)}) collective-permute-start(f32[256]{0:T(256)S(1)} %get-tuple-element.357), channel_id=1, source_target_pairs={{8,0},{16,8},{24,16},{32,24},{40,32},{48,40},{56,48},{64,56},{72,6... | collective-permute-start | bytes 3080 | tf_op jit(solution)/shard_map/ppermute | solution.py:20
  190.5 0.6 stack.5
  191.1 5.7 %all-to-all-start.1 = ((f32[8,5,256]{2,1,0:T(8,128)}), f32[8,5,256]{2,1,0:T(8,128)S(1)}, u32[]{:S(2)}, u32[]{:S(2)}) async-start(f32[8,5,256]{2,1,0:T(8,128)} %stack.5), calls=%async_computation.1 | async-start | bytes 131072 | tf_op jit(solution)/shard_map/all_to_all | solution.py:64
  196.8 65.3 %gather_fusion.5 = f32[16384]{0:T(1024)S(1)} fusion(f32[768]{0:T(1024)S(1)} %pad_maximum_fusion.4, s32[16384]{0:T(1024)S(1)} %broadcast_clamp_fusion), kind=kCustom, calls=%fused_computation.5 | custom fusion | bytes 196608 | tf_op jit(solution)/shard_map/gather | solution.py:71
  262.2 2.8 %while.33 = (s32[]{:T(128)}, f32[256]{0:T(256)S(1)}, f32[256]{0:T(256)S(1)}, f32[3,256]{1,0:T(4,128)S(1)}, f32[3,2048]{1,0:T(4,128)S(1)}, /*index=5*/f32[2048]{0...) while((s32[]{:T(128)}, f32[256]{0:T(256)S(1)}, ...), condition=%wide.region_9.0_spmd.clone, body=%wide.region_6.0_spmd.clone.sunk | while | flops 1704457 | bytes 48361 | solution.py:45
  262.5 0.4 multiply_reduce_fusion.8
  263.2 0.4 multiply_reduce_fusion.8
  263.9 0.4 multiply_reduce_fusion.8
  264.6 0.4 multiply_reduce_fusion.8
  265.0 0.6 fusion.7
  (85 shorter events, 2.4 us)
Async XLA Ops:
  1.4 0.7 copy-start
  5.6 16.0 %copy-start.3 = (f32[3,256]{1,0:T(4,128)S(1)}, f32[3,256]{1,0:T(4,128)}, u32[]{:S(2)}) copy-start(f32[3,256]{1,0:T(4,128)} %param.10) | copy-start | bytes 9220
  5.6 22.5 %collective-permute-start = (f32[256]{0:T(256)S(1)}, f32[256]{0:T(256)S(1)}, u32[]{:S(2)}, u32[]{:S(2)}) collective-permute-start(f32[256]{0:T(256)S(1)} %get-tuple-element.360), channel_id=1, source_target_pairs={{0,8},{8,16},{16,24},{24,32},{32,40},{40,48},{48,56},{56,64},{64,7... | collective-permute-start | bytes 3080 | tf_op jit(solution)/shard_map/ppermute | solution.py:18
  7.5 20.6 %collective-permute-start.1 = (f32[256]{0:T(256)S(1)}, f32[256]{0:T(256)S(1)}, u32[]{:S(2)}, u32[]{:S(2)}) collective-permute-start(f32[256]{0:T(256)S(1)} %get-tuple-element.361), channel_id=1, source_target_pairs={{8,0},{16,8},{24,16},{32,24},{40,32},{48,40},{56,48},{64,56},{72,6... | collective-permute-start | bytes 3080 | tf_op jit(solution)/shard_map/ppermute | solution.py:20
  21.6 0.7 copy-start.5
  22.9 5.1 %copy-start.4 = (s32[64,256]{1,0:T(8,128)S(1)}, s32[64,256]{1,0:T(8,128)}, u32[]{:S(2)}) copy-start(s32[64,256]{1,0:T(8,128)} %param.14) | copy-start | bytes 196612
  22.9 71.4 %all-to-all-start = ((f32[8,5,256]{2,1,0:T(8,128)}), f32[8,5,256]{2,1,0:T(8,128)S(1)}, u32[]{:S(2)}, u32[]{:S(2)}) async-start(f32[8,5,256]{2,1,0:T(8,128)} %stack.4), calls=%async_computation | async-start | bytes 131072 | tf_op jit(solution)/shard_map/all_to_all | solution.py:64
  93.4 0.8 copy-start.2
  100.7 9.8 %collective-permute-start.2 = (f32[256]{0:T(256)S(1)}, f32[256]{0:T(256)S(1)}, u32[]{:S(2)}, u32[]{:S(2)}) collective-permute-start(f32[256]{0:T(256)S(1)} %get-tuple-element.358), channel_id=1, source_target_pairs={{0,8},{8,16},{16,24},{24,32},{32,40},{40,48},{48,56},{56,64},{64,7... | collective-permute-start | bytes 3080 | tf_op jit(solution)/shard_map/ppermute | solution.py:18
  102.6 9.1 %collective-permute-start.3 = (f32[256]{0:T(256)S(1)}, f32[256]{0:T(256)S(1)}, u32[]{:S(2)}, u32[]{:S(2)}) collective-permute-start(f32[256]{0:T(256)S(1)} %get-tuple-element.359), channel_id=1, source_target_pairs={{8,0},{16,8},{24,16},{32,24},{40,32},{48,40},{56,48},{64,56},{72,6... | collective-permute-start | bytes 3080 | tf_op jit(solution)/shard_map/ppermute | solution.py:20
  177.1 87.9 %copy-start.1 = (f32[256]{0:T(256)}, f32[256]{0:T(256)S(1)}, u32[]{:S(2)}) copy-start(f32[256]{0:T(256)S(1)} %multiply_add_fusion) | copy-start | bytes 3076
  180.7 16.1 %collective-permute-start.4 = (f32[256]{0:T(256)S(1)}, f32[256]{0:T(256)S(1)}, u32[]{:S(2)}, u32[]{:S(2)}) collective-permute-start(f32[256]{0:T(256)S(1)} %get-tuple-element.356), channel_id=1, source_target_pairs={{0,8},{8,16},{16,24},{24,32},{32,40},{40,48},{48,56},{56,64},{64,7... | collective-permute-start | bytes 3080 | tf_op jit(solution)/shard_map/ppermute | solution.py:18
  182.6 14.2 %collective-permute-start.5 = (f32[256]{0:T(256)S(1)}, f32[256]{0:T(256)S(1)}, u32[]{:S(2)}, u32[]{:S(2)}) collective-permute-start(f32[256]{0:T(256)S(1)} %get-tuple-element.357), channel_id=1, source_target_pairs={{8,0},{16,8},{24,16},{32,24},{40,32},{48,40},{56,48},{64,56},{72,6... | collective-permute-start | bytes 3080 | tf_op jit(solution)/shard_map/ppermute | solution.py:20
  191.1 71.1 %all-to-all-start.1 = ((f32[8,5,256]{2,1,0:T(8,128)}), f32[8,5,256]{2,1,0:T(8,128)S(1)}, u32[]{:S(2)}, u32[]{:S(2)}) async-start(f32[8,5,256]{2,1,0:T(8,128)} %stack.5), calls=%async_computation.1 | async-start | bytes 131072 | tf_op jit(solution)/shard_map/all_to_all | solution.py:64
